TPU v7x, 32 devices: a whole 2x2x4 slice. The times are simulated.
32 devices in a mesh: row: 4 (over y, x), col: 8 (over z, core).
Axes of the slice: x: 2, y: 2, z: 4, core: 2. Of those that a mesh axis runs over, the one named last changes fastest.
Arguments:
- tokens: bfloat16 [1024, 53248], P(('row', 'col')), may hold values from -6 to 6
- eigvecs: float32 [53248, 2048], P('row', 'col'), may hold values from -0.02734375 to 0.02734375
- eigvals: float32 [2048], P('col'), may hold values from 0.25 to 4
- v_first: float32 [53248, 256], P(('row', 'col')), may hold values from -0.109375 to 0.109375
- v_second: float32 [53248, 256], P(('row', 'col')), may hold values from -0.109375 to 0.109375
- t_first: float32 [256, 256], replicated, may hold values from -0.375 to 0.375
- t_second: float32 [256, 256], replicated, may hold values from -0.375 to 0.375
Outputs:
- whitened: float32 [1024, 2048], P('row', 'col')
All inputs are finite; a program needn't handle non-finite values.
Results may differ from a plain program's by a relative error of at most 0.0029.
Values may be sent and summed in bfloat16 or wider, within the bound.
No kernel may reach another device: no remote copies, remote signals or barrier semaphores. Data moves between devices by JAX's collectives and lax.ppermute only.
A program may use at most 128 MiB of HBM per device.

v0:
```python
import jax
import jax.numpy as jnp
from jax import lax
from jax.sharding import PartitionSpec as P


def local_update(block, panel, factor, inner):
    middle = jnp.dot(
        factor, inner, precision=lax.Precision.HIGHEST, preferred_element_type=jnp.float32
    )
    return block - jnp.dot(
        panel, middle, precision=lax.Precision.HIGHEST, preferred_element_type=jnp.float32
    )


def partial_inner(panel, block):
    return jnp.dot(
        panel.T, block, precision=lax.Precision.HIGHEST, preferred_element_type=jnp.float32
    )


def per_device(tokens, eigvecs, eigvals, v_first, v_second, t_first, t_second):
    block = lax.all_to_all(eigvecs, "col", split_axis=0, concat_axis=1, tiled=True)
    for panel, factor in ((v_second, t_second), (v_first, t_first)):
        inner = lax.psum(partial_inner(panel, block), ("row", "col"))
        block = local_update(block, panel, factor, inner)
    every_value = lax.all_gather(eigvals, "col", axis=0, tiled=True)
    whitening = (block * lax.rsqrt(every_value)[None, :]).astype(jnp.bfloat16)
    slab = lax.all_to_all(tokens, ("row", "col"), split_axis=1, concat_axis=0, tiled=True)
    partial_value = jnp.dot(slab, whitening, preferred_element_type=jnp.float32)
    by_column = lax.psum_scatter(partial_value, "col", scatter_dimension=1, tiled=True)
    summed = lax.psum_scatter(by_column, "row", scatter_dimension=0, tiled=True)
    return summed


def solution(mesh):
    in_specs = (
        P(("row", "col"), None),
        P("row", "col"),
        P("col"),
        P(("row", "col"), None),
        P(("row", "col"), None),
        P(),
        P(),
    )
    out_specs = P("row", "col")
    return jax.shard_map(
        per_device, mesh=mesh, in_specs=in_specs, out_specs=out_specs, check_vma=False
    )
```

profile of v0, /device:TPU:0, one launch (start us, length us, event | category | flops | bytes accessed | tf_op | source)
XLA Modules:
  0.0 837.7 jit_solution(9575933095389601247)
XLA Ops:
  6.5 13.8 %copy.15 = f32[8,1664,256]{1,2,0:T(8,128)} copy(f32[8,1664,256]{2,1,0:T(8,128)} %bitcast.39) | data formatting | bytes 27262976 | tf_op jit(solution)/shard_map/all_to_all | solution.py:23
  20.4 6.4 all-to-all-start
  26.7 4.1 copy.20
  30.8 292.2 %all-to-all-done = f32[8,1664,256]{1,2,0:T(8,128)} async-done(((f32[8,1664,256]{1,2,0:T(8,128)}), f32[8,1664,256]{1,2,0:T(8,128)}, u32[]{:S(2)}, u32[]{:S(2)}) %all-to-all-start) | async-done | bytes 13631520 | tf_op jit(solution)/shard_map/all_to_all | solution.py:23
  323.0 4.1 all-to-all-start.1
  327.2 0.0 all-reduce.3.cloned.1.call-start
  327.2 25.8 %fusion.2 = f32[256,2048]{1,0:T(8,128)} fusion(f32[1664,256]{1,0:T(8,128)S(1)} %copy-done, f32[1664,2048]{0,1:T(8,128)} %bitcast.2), kind=kOutput, calls=%fused_computation.7 | convolution fusion | flops 10468982784 | bytes 17432576 | tf_op jit(solution)/shard_map/dot_general | solution.py:17
  353.1 0.2 all-reduce.5.cloned.1.call-start
  353.3 151.8 %all-reduce.3.cloned.1.call-done = f32[256,2048]{1,0:T(8,128)} async-done(((f32[256,2048]{1,0:T(8,128)}), f32[256,2048]{1,0:T(8,128)}) %all-reduce.3.cloned.1.call-update) | async-done | bytes 2097168 | tf_op jit(solution)/shard_map/psum | solution.py:25
  505.2 5.2 fusion.3
  510.3 16.9 %bitcast_subtract_fusion.1 = f32[1664,2048]{0,1:T(8,128)S(1)} fusion(f32[1664,2048]{0,1:T(8,128)} %bitcast.2, f32[2048,256]{1,0:T(8,128)S(1)} %fusion.3, f32[1664,256]{1,0:T(8,128)S(1)} %copy-done), kind=kOutput, calls=%fused_computation.3 | convolution fusion | flops 10472390656 | bytes 31064064 | tf_op jit(solution)/shard_map/dot_general | solution.py:11
  527.3 4.9 copy-done.2
  532.1 13.1 %convolution_bitcast_fusion.1 = f32[256,2048]{0,1:T(8,128)} fusion(f32[1664,2048]{0,1:T(8,128)S(1)} %bitcast_subtract_fusion.1, f32[1664,256]{1,0:T(8,128)S(1)} %copy-done.3), kind=kOutput, calls=%fused_computation.6 | convolution fusion | flops 10468982784 | bytes 17432576 | tf_op jit(solution)/shard_map/dot_general | solution.py:17
  545.3 0.0 reduce-scatter.3.cloned.1.call-start
  545.4 0.6 copy-done.6
  546.0 10.6 %all-gather = f32[8,1,256]{2,1,0:T(1,128)S(1)} all-gather(f32[1,1,256]{2,1,0:T(1,128)S(1)} %bitcast.43), channel_id=1, replica_groups=mesh['row'=4,'col'=8] {'col'}, dimensions={0}, use_global_device_ids=true | all-gather | bytes 9216 | tf_op jit(solution)/shard_map/all_gather | solution.py:27
  556.6 122.3 %all-reduce.5.cloned.1.call-done = f32[256,2048]{0,1:T(8,128)} async-done(((f32[256,2048]{0,1:T(8,128)}), f32[256,2048]{0,1:T(8,128)}) %all-reduce.5.cloned.1.call-update) | async-done | bytes 2097168 | tf_op jit(solution)/shard_map/psum | solution.py:25
  678.9 3.5 fusion.4
  682.4 16.4 %fusion.1 = bf16[1664,2048]{0,1:T(8,128)(2,1)} fusion(f32[1664,2048]{0,1:T(8,128)} %copy-done.2, f32[2048,256]{1,0:T(8,128)S(1)} %fusion.4, f32[1664,256]{1,0:T(8,128)S(1)} %copy-done.3, f32[2048]{0:T(1024)S(1)} %bitcast.42), kind=kOutput, calls=%fused_computation.2 | convolution fusion | flops 10479206400 | bytes 24256512 | tf_op jit(solution)/shard_map/dot_general | solution.py:11
  698.8 12.9 %convolution_bitcast_fusion = f32[1024,2048]{0,1:T(8,128)} fusion(bf16[1664,2048]{0,1:T(8,128)(2,1)} %fusion.1, bf16[1024,1664]{1,0:T(8,128)(2,1)} %bitcast.10), kind=kOutput, calls=%fused_computation.4 | convolution fusion | flops 6979321856 | bytes 18612224 | tf_op jit(solution)/shard_map/dot_general | solution.py:30
  711.8 0.0 reduce-scatter.5.cloned.1.call-start
  711.9 88.4 %reduce-scatter.3.cloned.1.call-done = f32[1024,256]{0,1:T(8,128)} async-done(((f32[1024,2048]{0,1:T(8,128)}), f32[1024,256]{0,1:T(8,128)}) %reduce-scatter.3.cloned.1.call-update) | async-done | bytes 1048592 | tf_op jit(solution)/shard_map/reduce_scatter | solution.py:31
  800.2 29.2 %reduce-scatter.5.cloned.1.call-done = f32[256,256]{0,1:T(8,128)} async-done(((f32[1024,256]{0,1:T(8,128)}), f32[256,256]{0,1:T(8,128)}) %reduce-scatter.5.cloned.1.call-update) | async-done | bytes 262160 | tf_op jit(solution)/shard_map/reduce_scatter | solution.py:32
  829.4 1.8 copy.17
  (18 shorter events, 0.1 us)
Async XLA Ops:
  6.5 320.7 %copy-start = (f32[1664,256]{1,0:T(8,128)S(1)}, f32[1664,256]{1,0:T(8,128)}, u32[]{:S(2)}) copy-start(f32[1664,256]{1,0:T(8,128)} %param.11) | copy-start | bytes 5111812
  20.4 302.7 %all-to-all-start = ((f32[8,1664,256]{1,2,0:T(8,128)}), f32[8,1664,256]{1,2,0:T(8,128)}, u32[]{:S(2)}, u32[]{:S(2)}) async-start(f32[8,1664,256]{1,2,0:T(8,128)} %copy.15), calls=%async_computation | async-start | bytes 27262976 | tf_op jit(solution)/shard_map/all_to_all | solution.py:23
  323.0 375.8 %all-to-all-start.1 = ((bf16[32,32,1664]{2,0,1:T(8,128)(2,1)}), bf16[32,32,1664]{2,0,1:T(8,128)(2,1)}, u32[]{:S(2)}, u32[]{:S(2)}) async-start(bf16[32,32,1664]{2,0,1:T(8,128)(2,1)} %bitcast.40), calls=%async_computation.1 | async-start | bytes 6815744 | tf_op jit(solution)/shard_map/all_to_all | solution.py:29
  327.2 178.0 %all-reduce.3.cloned.1.call-start = ((), (), s32[]{:S(2)}) async-start(), calls=%async_computation.4 | async-start | bytes 4194304 | tf_op jit(solution)/shard_map/psum | solution.py:25
  353.1 152.1 %copy-start.4 = (f32[256,256]{1,0:T(8,128)S(1)}, f32[256,256]{1,0:T(8,128)}, u32[]{:S(2)}) copy-start(f32[256,256]{1,0:T(8,128)} %param.13) | copy-start | bytes 786436
  353.1 325.8 %all-reduce.5.cloned.1.call-start = ((), (), s32[]{:S(2)}) async-start(), calls=%async_computation.5 | async-start | bytes 4194304 | tf_op jit(solution)/shard_map/psum | solution.py:25
  510.3 21.8 %copy-start.3 = (f32[1664,256]{1,0:T(8,128)S(1)}, f32[1664,256]{1,0:T(8,128)}, u32[]{:S(2)}) copy-start(f32[1664,256]{1,0:T(8,128)} %param.10) | copy-start | bytes 5111812
  527.2 4.9 copy-start.2
  545.3 0.7 copy-start.6
  545.3 133.6 %copy-start.5 = (f32[256,256]{1,0:T(8,128)S(1)}, f32[256,256]{1,0:T(8,128)}, u32[]{:S(2)}) copy-start(f32[256,256]{1,0:T(8,128)} %param.12) | copy-start | bytes 786436
  545.3 254.9 %reduce-scatter.3.cloned.1.call-start = ((), (), s32[]{:S(2)}) async-start(), calls=%async_computation.6 | async-start | bytes 9437184 | tf_op jit(solution)/shard_map/reduce_scatter | solution.py:31
  711.8 119.4 %copy-start.1 = (f32[1664,256]{1,0:T(8,128)S(1)}, f32[1664,256]{1,0:T(8,128)}, u32[]{:S(2)}) copy-start(f32[1664,256]{1,0:T(8,128)} %param.11) | copy-start | bytes 5111812
  711.8 117.6 %reduce-scatter.5.cloned.1.call-start = ((), (), s32[]{:S(2)}) async-start(), calls=%async_computation.7 | async-start | bytes 1310720 | tf_op jit(solution)/shard_map/reduce_scatter | solution.py:32
Sparse Core Ops, SparseCore 0:
  353.2 151.8 all-reduce.2
  545.4 133.4 all-reduce.4
  711.9 88.2 reduce-scatter.2
  803.0 26.4 reduce-scatter.4
where the time goes:
time: 838 us
  waiting for transfers between devices  684 us (82%)
  matrix products  93.9 us (11%)
  local copies, waits for them, and re-layouts  25.3 us (3%)
  between operations  13.2 us (2%)
  starting transfers between devices  10.8 us (1%)
  blocking collectives  10.6 us (1%)
    all_to_all x1, waiting for transfers between devices, per_device(): lax.all_to_all(eigvecs, 'col', split_axis=0, concat_axis=1, tiled=True)  292 us
    psum x2, waiting for transfers between devices, per_device(): inner = lax.psum(partial_inner(panel, block), ('row', 'col'))  274 us
    reduce_scatter x1, waiting for transfers between devices, per_device(): lax.psum_scatter(partial_value, 'col', scatter_dimension=1, tiled=True)  88.4 us
    dot_general x2, matrix products, partial_inner(): jnp.dot(panel.T, block, precision=lax.Precision.HIGHEST, preferred_elemen...  39 us
    dot_general x2, matrix products, local_update(): jnp.dot(panel, middle, precision=lax.Precision.HIGHEST, preferred_element...  33.3 us
    reduce_scatter x1, waiting for transfers between devices, per_device(): summed = lax.psum_scatter(by_column, 'row', scatter_dimension=0, tiled=True)  29.2 us
  transfers between devices with their start and end apart: 6, of which 5 were waited for; matrix products, arithmetic and copies ran while one was open for 10% of the time, Pallas kernels for 0%

commit v1 on v0

--- a/solution.py
+++ b/solution.py
@@ -22,7 +22,11 @@
 def per_device(tokens, eigvecs, eigvals, v_first, v_second, t_first, t_second):
     block = lax.all_to_all(eigvecs, "col", split_axis=0, concat_axis=1, tiled=True)
     for panel, factor in ((v_second, t_second), (v_first, t_first)):
-        inner = lax.psum(partial_inner(panel, block), ("row", "col"))
+
+        def remake_regions(message):
+            return lax.psum(lax.psum(message, axis_name="row"), axis_name="col")
+
+        inner = remake_regions(partial_inner(panel, block))
         block = local_update(block, panel, factor, inner)
     every_value = lax.all_gather(eigvals, "col", axis=0, tiled=True)
     whitening = (block * lax.rsqrt(every_value)[None, :]).astype(jnp.bfloat16)

time: 838 us -> 891 us (1.063); the launches traced: 838 us -> 881 us
  blocking collectives: 10.6 us -> 315 us
  waiting for transfers between devices: 684 us -> 426 us
    all_to_all x0 -> x1, blocking collectives: none -> 303 us  [per_device(): lax.all_to_all(eigvecs, 'col', split_axis=0, concat_axis=1, tiled=True)]
    all_to_all x1 -> x0, waiting for transfers between devices: 292 us -> none  [per_device(): lax.all_to_all(eigvecs, 'col', split_axis=0, concat_axis=1, tiled=True)]
    psum x2 -> x4, waiting for transfers between devices: 274 us -> 308 us  [remake_regions(): return lax.psum(lax.psum(message, axis_name='row'), axis_name='col')]
  transfers between devices with their start and end apart: 6 -> 7, of which waited for: 5 -> 6; matrix products, arithmetic and copies ran while one was open for 10% -> 7% of each run, Pallas kernels for 0% -> 0%
where the time goes in v1:
time: 891 us; the launch traced here: 881 us
  waiting for transfers between devices  426 us (48%)
  blocking collectives  315 us (35%)
  matrix products  91.7 us (10%)
  local copies, waits for them, and re-layouts  29.5 us (3%)
  between operations  14 us (2%)
    psum x4, waiting for transfers between devices, remake_regions(): return lax.psum(lax.psum(message, axis_name='row'), axis_name='col')  308 us
    all_to_all x1, blocking collectives, per_device(): lax.all_to_all(eigvecs, 'col', split_axis=0, concat_axis=1, tiled=True)  303 us
    reduce_scatter x1, waiting for transfers between devices, per_device(): lax.psum_scatter(partial_value, 'col', scatter_dimension=1, tiled=True)  89.2 us
    dot_general x2, matrix products, partial_inner(): jnp.dot(panel.T, block, precision=lax.Precision.HIGHEST, preferred_elemen...  36.5 us
    dot_general x2, matrix products, local_update(): jnp.dot(panel, middle, precision=lax.Precision.HIGHEST, preferred_element...  33.5 us
    reduce_scatter x1, waiting for transfers between devices, per_device(): summed = lax.psum_scatter(by_column, 'row', scatter_dimension=0, tiled=True)  29.2 us
  transfers between devices with their start and end apart: 7, of which 6 were waited for; matrix products, arithmetic and copies ran while one was open for 7% of the time, Pallas kernels for 0%

profile of v1, /device:TPU:0, one launch (start us, length us, event | category | flops | bytes accessed | tf_op | source)
XLA Modules:
  0.0 881.1 jit_solution(1540341761491862977)
XLA Ops:
  6.5 13.9 %copy.15 = f32[8,1664,256]{1,2,0:T(8,128)} copy(f32[8,1664,256]{2,1,0:T(8,128)} %bitcast.41) | data formatting | bytes 27262976 | tf_op jit(solution)/shard_map/all_to_all | solution.py:23
  20.4 302.6 %all_to_all.38 = f32[8,1664,256]{1,2,0:T(8,128)S(1)} all-to-all(f32[8,1664,256]{1,2,0:T(8,128)} %copy.15), channel_id=1, replica_groups=mesh['row'=4,'col'=8] {'col'}, dimensions={0} | all-to-all | bytes 27262976 | tf_op jit(solution)/shard_map/all_to_all | solution.py:23
  323.0 4.9 copy-done.3
  327.9 23.4 %fusion.2 = f32[256,2048]{1,0:T(8,128)} fusion(f32[1664,256]{1,0:T(8,128)S(1)} %copy-done, f32[1664,2048]{0,1:T(8,128)S(1)} %bitcast.39), kind=kOutput, calls=%fused_computation.7 | convolution fusion | flops 10468982784 | bytes 17432576 | tf_op jit(solution)/shard_map/dot_general | solution.py:17
  351.3 0.0 all-reduce.7.cloned.1.call-start
  351.4 68.5 %all-reduce.5.cloned.1.call-done = f32[256,2048]{1,0:T(8,128)} async-done(((f32[256,2048]{1,0:T(8,128)}), f32[256,2048]{1,0:T(8,128)}) %all-reduce.5.cloned.1.call-update) | async-done | bytes 2097168 | tf_op jit(solution)/shard_map/psum | solution.py:27
  419.9 4.0 copy.20
  423.9 4.7 all-to-all-start.1
  428.7 0.0 all-reduce.9.cloned.1.call-start
  428.7 115.5 %all-reduce.7.cloned.1.call-done = f32[256,2048]{1,0:T(8,128)} async-done(((f32[256,2048]{1,0:T(8,128)}), f32[256,2048]{1,0:T(8,128)}) %all-reduce.7.cloned.1.call-update) | async-done | bytes 2097168 | tf_op jit(solution)/shard_map/psum | solution.py:27
  544.2 5.2 fusion.3
  549.4 17.1 %bitcast_subtract_fusion.1 = f32[1664,2048]{0,1:T(8,128)S(1)} fusion(f32[1664,2048]{0,1:T(8,128)} %bitcast.40, f32[2048,256]{1,0:T(8,128)S(1)} %fusion.3, f32[1664,256]{1,0:T(8,128)S(1)} %copy-done), kind=kOutput, calls=%fused_computation.3 | convolution fusion | flops 10472390656 | bytes 31064064 | tf_op jit(solution)/shard_map/dot_general | solution.py:11
  566.5 4.9 copy-done.2
  571.4 13.1 %convolution_bitcast_fusion.1 = f32[256,2048]{0,1:T(8,128)} fusion(f32[1664,2048]{0,1:T(8,128)S(1)} %bitcast_subtract_fusion.1, f32[1664,256]{1,0:T(8,128)S(1)} %copy-done.4), kind=kOutput, calls=%fused_computation.6 | convolution fusion | flops 10468982784 | bytes 17432576 | tf_op jit(solution)/shard_map/dot_general | solution.py:17
  584.6 68.7 %all-reduce.9.cloned.1.call-done = f32[256,2048]{0,1:T(8,128)} async-done(((f32[256,2048]{0,1:T(8,128)}), f32[256,2048]{0,1:T(8,128)}) %all-reduce.9.cloned.1.call-update) | async-done | bytes 2097168 | tf_op jit(solution)/shard_map/psum | solution.py:27
  653.3 12.0 %all-gather = f32[8,1,256]{2,1,0:T(1,128)S(1)} all-gather(f32[1,1,256]{2,1,0:T(1,128)S(1)} %bitcast.45), channel_id=1, replica_groups=mesh['row'=4,'col'=8] {'col'}, dimensions={0}, use_global_device_ids=true | all-gather | bytes 9216 | tf_op jit(solution)/shard_map/all_gather | solution.py:31
  665.4 55.3 %all-reduce.11.cloned.1.call-done = f32[256,2048]{0,1:T(8,128)} async-done(((f32[256,2048]{0,1:T(8,128)}), f32[256,2048]{0,1:T(8,128)}) %all-reduce.11.cloned.1.call-update) | async-done | bytes 2097168 | tf_op jit(solution)/shard_map/psum | solution.py:27
  720.6 3.5 fusion.4
  724.1 16.4 %fusion.1 = bf16[1664,2048]{0,1:T(8,128)(2,1)} fusion(f32[1664,2048]{0,1:T(8,128)} %copy-done.2, f32[2048,256]{1,0:T(8,128)S(1)} %fusion.4, f32[1664,256]{1,0:T(8,128)S(1)} %copy-done.4, f32[2048]{0:T(1024)S(1)} %bitcast.44), kind=kOutput, calls=%fused_computation.2 | convolution fusion | flops 10479206400 | bytes 24256512 | tf_op jit(solution)/shard_map/dot_general | solution.py:11
  740.6 12.9 %convolution_bitcast_fusion = f32[1024,2048]{0,1:T(8,128)} fusion(bf16[1664,2048]{0,1:T(8,128)(2,1)} %fusion.1, bf16[1024,1664]{1,0:T(8,128)(2,1)} %bitcast.10), kind=kOutput, calls=%fused_computation.4 | convolution fusion | flops 6979321856 | bytes 18612224 | tf_op jit(solution)/shard_map/dot_general | solution.py:34
  753.5 0.0 reduce-scatter.5.cloned.1.call-start
  753.6 89.2 %reduce-scatter.3.cloned.1.call-done = f32[1024,256]{0,1:T(8,128)} async-done(((f32[1024,2048]{0,1:T(8,128)}), f32[1024,256]{0,1:T(8,128)}) %reduce-scatter.3.cloned.1.call-update) | async-done | bytes 1048592 | tf_op jit(solution)/shard_map/reduce_scatter | solution.py:35
  842.9 29.2 %reduce-scatter.5.cloned.1.call-done = f32[256,256]{0,1:T(8,128)} async-done(((f32[1024,256]{0,1:T(8,128)}), f32[256,256]{0,1:T(8,128)}) %reduce-scatter.5.cloned.1.call-update) | async-done | bytes 262160 | tf_op jit(solution)/shard_map/reduce_scatter | solution.py:36
  872.0 1.8 copy.17
  (25 shorter events, 0.2 us)
Async XLA Ops:
  6.5 321.3 %copy-start = (f32[1664,256]{1,0:T(8,128)S(1)}, f32[1664,256]{1,0:T(8,128)}, u32[]{:S(2)}) copy-start(f32[1664,256]{1,0:T(8,128)} %param.11) | copy-start | bytes 5111812
  6.5 413.4 %all-reduce.5.cloned.1.call-start = ((), (), s32[]{:S(2)}) async-start(), calls=%async_computation.4 | async-start | bytes 4194304 | tf_op jit(solution)/shard_map/psum | solution.py:27
  323.0 4.9 copy-start.3
  351.3 192.9 %all-reduce.7.cloned.1.call-start = ((), (), s32[]{:S(2)}) async-start(), calls=%async_computation.5 | async-start | bytes 4194304 | tf_op jit(solution)/shard_map/psum | solution.py:27
  423.9 120.3 %copy-start.5 = (f32[256,256]{1,0:T(8,128)S(1)}, f32[256,256]{1,0:T(8,128)}, u32[]{:S(2)}) copy-start(f32[256,256]{1,0:T(8,128)} %param.13) | copy-start | bytes 786436
  423.9 316.6 %all-to-all-start.1 = ((bf16[32,32,1664]{2,0,1:T(8,128)(2,1)}), bf16[32,32,1664]{2,0,1:T(8,128)(2,1)}, u32[]{:S(2)}, u32[]{:S(2)}) async-start(bf16[32,32,1664]{2,0,1:T(8,128)(2,1)} %bitcast.42), calls=%async_computation.1 | async-start | bytes 6815744 | tf_op jit(solution)/shard_map/all_to_all | solution.py:33
  428.7 224.6 %all-reduce.9.cloned.1.call-start = ((), (), s32[]{:S(2)}) async-start(), calls=%async_computation.6 | async-start | bytes 4194304 | tf_op jit(solution)/shard_map/psum | solution.py:27
  549.4 22.0 %copy-start.4 = (f32[1664,256]{1,0:T(8,128)S(1)}, f32[1664,256]{1,0:T(8,128)}, u32[]{:S(2)}) copy-start(f32[1664,256]{1,0:T(8,128)} %param.10) | copy-start | bytes 5111812
  566.5 4.9 copy-start.2
  584.5 68.8 %copy-start.7 = (f32[256]{0:T(256)S(1)}, f32[256]{0:T(256)}, u32[]{:S(2)}) copy-start(f32[256]{0:T(256)} %param.9) | copy-start | bytes 3076
  584.5 136.1 %copy-start.6 = (f32[256,256]{1,0:T(8,128)S(1)}, f32[256,256]{1,0:T(8,128)}, u32[]{:S(2)}) copy-start(f32[256,256]{1,0:T(8,128)} %param.12) | copy-start | bytes 786436
  584.6 136.1 %all-reduce.11.cloned.1.call-start = ((), (), s32[]{:S(2)}) async-start(), calls=%async_computation.7 | async-start | bytes 4194304 | tf_op jit(solution)/shard_map/psum | solution.py:27
  653.3 189.5 %reduce-scatter.3.cloned.1.call-start = ((), (), s32[]{:S(2)}) async-start(), calls=%async_computation.8 | async-start | bytes 9437184 | tf_op jit(solution)/shard_map/reduce_scatter | solution.py:35
  753.5 120.3 %copy-start.1 = (f32[1664,256]{1,0:T(8,128)S(1)}, f32[1664,256]{1,0:T(8,128)}, u32[]{:S(2)}) copy-start(f32[1664,256]{1,0:T(8,128)} %param.11) | copy-start | bytes 5111812
  753.5 118.5 %reduce-scatter.5.cloned.1.call-start = ((), (), s32[]{:S(2)}) async-start(), calls=%async_computation.9 | async-start | bytes 1310720 | tf_op jit(solution)/shard_map/reduce_scatter | solution.py:36
Sparse Core Ops, SparseCore 0:
  351.4 68.4 all-reduce.4
  422.3 121.9 all-reduce.6
  584.7 68.5 all-reduce.8
  655.5 65.0 all-reduce.10
  753.7 89.1 reduce-scatter.2
  845.6 26.4 reduce-scatter.4
